TPU v7x, 128 devices: a whole 4x4x4 slice. The times are simulated.
128 devices in a mesh: vox: 8 (over y, core), fas: 16 (over z, x).
Axes of the slice: x: 4, y: 4, z: 4, core: 2. Of those that a mesh axis runs over, the one named last changes fastest.
Arguments:
- signal: float32 [128, 6144], P('vox', 'fas'), may hold values from -6 to 6
- initial_weights: float32 [524288], P('fas'), may hold values from 0.1 to 2
- coefficients: bfloat16 [32768, 4096], P(('vox', 'fas')), may hold values from 0 to 0.0234375
- block_rows: int32 [32768], P(('vox', 'fas')), may hold values from 0 to 127, as said below
- block_cols: int32 [32768], P(('vox', 'fas')), may hold values from 0 to 8191, as said below
- block_atoms: int32 [32768, 64], P(('vox', 'fas')), may hold values from 0 to 359
- block_count: int32 [128], P(('vox', 'fas')), may hold values from 64 to 256, as said below
- dictionary: bfloat16 [360, 96], replicated, may hold values from -6 to 6
Outputs:
- weights: float32 [524288], P('fas')
- residual: float32 [128, 6144], P('vox', 'fas')
Inputs may be any that keep to these rules, and one draw needn't show every extreme that they name: Block slots are stored device by device: the device with vox index i and fas index f holds slots (i * 16 + f) * 256 to (i * 16 + f + 1) * 256 - 1, and every block_rows value there lies in i * 16 to (i + 1) * 16 - 1. For the slots of the device with fas index f, every block_cols value lies in f * 512 to (f + 1) * 512 - 1. `block_count`: entry i * 16 + f is the number of live slots of the device with vox index i and fas index f, its first slots; some device has all 256 live.
All inputs are finite; a program needn't handle non-finite values.
Results may differ from a plain program's by a relative error of at most 0.0003.
Values sent between devices are 32-bit elements; how exact they have to be, the bound alone decides.
A program may use at most 128 MiB of HBM per device.

v0:
```python
import jax
import jax.numpy as jnp
from jax import lax
from jax.sharding import PartitionSpec as P

BV = 64
BF = 64
DIRS = 96
ITERS = 5


def local(
    signal,
    initial_weights,
    coefficients,
    block_rows,
    block_cols,
    block_atoms,
    block_count,
    dictionary,
):
    vox_rows = signal.shape[0]
    fas_rows = initial_weights.shape[0] // BF
    slot_total = coefficients.shape[0]
    row_width = BV * DIRS
    fas_place = lax.axis_index("fas")
    rows_local = block_rows - lax.axis_index("vox") * vox_rows
    cols_local = block_cols - fas_place * fas_rows
    live_count = block_count[0]
    atom_table = dictionary[block_atoms]
    coef_view = coefficients.reshape(slot_total, BV, BF)
    group_size = min(256, slot_total)
    group_turns = (live_count + group_size - 1) // group_size
    vox_range = jnp.arange(vox_rows, dtype=jnp.int32)
    fas_range = jnp.arange(fas_rows, dtype=jnp.int32)

    def group_pieces(first_slot):
        live_mask = (first_slot + jnp.arange(group_size, dtype=jnp.int32) < live_count).astype(
            jnp.float32
        )
        return (coef_view, atom_table, rows_local, cols_local, live_mask)

    def forward_partial(values):
        table = values.reshape(fas_rows, BF)

        def forward_accumulate(turn, running):
            coef_blk, atom_blk, rows_blk, cols_blk, live_mask = group_pieces(turn * group_size)
            scaled = coef_blk.astype(jnp.float32) * table[cols_blk][:, None, :]
            image_blk = jnp.einsum(
                "kvj,kjd->kvd",
                scaled,
                atom_blk.astype(jnp.float32),
                precision=lax.Precision.HIGHEST,
                preferred_element_type=jnp.float32,
            )
            selector = (rows_blk[:, None] == vox_range[None, :]).astype(jnp.float32) * live_mask[
                :, None
            ]
            added = jnp.dot(
                selector.T,
                image_blk.reshape(group_size, row_width),
                precision=lax.Precision.HIGHEST,
                preferred_element_type=jnp.float32,
            )
            return running + added

        start = jnp.zeros((vox_rows, row_width), jnp.float32)
        return lax.fori_loop(0, group_turns, forward_accumulate, start)

    def backward_partial(rows_view):

        def backward_accumulate(turn, running):
            coef_blk, atom_blk, rows_blk, cols_blk, live_mask = group_pieces(turn * group_size)
            gathered = rows_view[rows_blk]
            inner = jnp.einsum(
                "kvj,kvd->kjd",
                coef_blk.astype(jnp.float32),
                gathered,
                precision=lax.Precision.HIGHEST,
                preferred_element_type=jnp.float32,
            )
            contrib = jnp.sum(atom_blk.astype(jnp.float32) * inner, axis=-1)
            selector = (cols_blk[:, None] == fas_range[None, :]).astype(jnp.float32) * live_mask[
                :, None
            ]
            added = jnp.dot(
                selector.T,
                contrib,
                precision=lax.Precision.HIGHEST,
                preferred_element_type=jnp.float32,
            )
            return running + added

        start = jnp.zeros((fas_rows, BF), jnp.float32)
        running = lax.fori_loop(0, group_turns, backward_accumulate, start)
        return running.reshape(-1)

    def collect(partial_value):
        return lax.psum_scatter(partial_value, "fas", scatter_dimension=1, tiled=True)

    weights = initial_weights
    residual = collect(forward_partial(weights)) - signal
    for sweep in range(ITERS):
        whole_rows = lax.all_gather(residual, "fas", axis=1, tiled=True)
        gradient = lax.psum(backward_partial(whole_rows.reshape(vox_rows, BV, DIRS)), "vox")
        projected = jnp.where((weights > 0) | (gradient < 0), gradient, 0.0)
        image_pred = collect(forward_partial(projected))
        image_local = jnp.sum(image_pred * image_pred)
        grad_sq = lax.psum(jnp.sum(projected * projected), "fas")
        image_sq = lax.psum(image_local, ("vox", "fas"))
        step_size = grad_sq / (image_sq + 1e-06)
        weights = jnp.maximum(weights - step_size * projected, 0.0)
        residual = collect(forward_partial(weights)) - signal
    return (weights, residual)


def solution(mesh):
    placed = (
        P("vox", "fas"),
        P("fas"),
        P(("vox", "fas"), None),
        P(("vox", "fas")),
        P(("vox", "fas")),
        P(("vox", "fas"), None),
        P(("vox", "fas")),
        P(),
    )
    return jax.shard_map(
        local, mesh=mesh, in_specs=placed, out_specs=(P("fas"), P("vox", "fas")), check_vma=False
    )
```

profile of v0, /device:TPU:0, one launch (start us, length us, event | category | flops | bytes accessed | tf_op | source)
XLA Modules:
  0.0 2227.8 jit_solution(15539309578874618926)
XLA Ops:
  18.6 57.4 %gather_fusion = bf16[16384,96]{1,0:T(8,128)(2,1)} fusion(bf16[360,96]{1,0:T(8,128)(2,1)S(1)} %copy.28, s32[16384]{0:T(1024)S(1)} %broadcast_clamp_fusion), kind=kCustom, calls=%fused_computation | custom fusion | bytes 6356992 | tf_op jit(solution)/shard_map/gather | solution.py:30
  105.5 74.3 %reduce-scatter.12.cloned.1.call-done = f32[16,384]{1,0:T(8,128)} async-done(((f32[16,6144]{1,0:T(8,128)}), f32[16,384]{1,0:T(8,128)}) %reduce-scatter.12.cloned.1.call-update) | async-done | bytes 24592 | tf_op jit(solution)/shard_map/reduce_scatter | solution.py:99
  224.2 58.0 %all-reduce.6.cloned.1.call-done = f32[32768]{0:T(1024)} async-done(((f32[32768]{0:T(1024)}), f32[32768]{0:T(1024)}) %all-reduce.6.cloned.1.call-update) | async-done | bytes 131088 | tf_op jit(solution)/shard_map/psum | solution.py:105
  313.8 70.8 %reduce-scatter.14.cloned.1.call-done = f32[16,384]{1,0:T(8,128)} async-done(((f32[16,6144]{1,0:T(8,128)}), f32[16,384]{1,0:T(8,128)}) %reduce-scatter.14.cloned.1.call-update) | async-done | bytes 24592 | tf_op jit(solution)/shard_map/reduce_scatter | solution.py:99
  386.1 38.8 %psum.106 = f32[]{:T(128)} all-reduce(f32[]{:T(128)} %get-tuple-element.2460), channel_id=1, replica_groups=mesh['vox'=8,'fas'=16] {'fas'}, use_global_device_ids=true, to_apply=%region_8.9 | all-reduce | flops 1 | bytes 8 | tf_op jit(solution)/shard_map/psum | solution.py:109
  424.8 62.7 %psum.107 = f32[]{:T(128)} all-reduce(f32[]{:T(128)} %multiply_reduce_fusion.9), channel_id=1, replica_groups=mesh['vox'=8,'fas'=16] {'vox','fas'}, use_global_device_ids=true, to_apply=%region_13.14 | all-reduce | flops 1 | bytes 8 | tf_op jit(solution)/shard_map/psum | solution.py:110
  518.7 69.0 %reduce-scatter.16.cloned.1.call-done = f32[16,384]{1,0:T(8,128)} async-done(((f32[16,6144]{1,0:T(8,128)}), f32[16,384]{1,0:T(8,128)}) %reduce-scatter.16.cloned.1.call-update) | async-done | bytes 24592 | tf_op jit(solution)/shard_map/reduce_scatter | solution.py:99
  632.2 58.0 %all-reduce.8.cloned.1.call-done = f32[32768]{0:T(1024)} async-done(((f32[32768]{0:T(1024)}), f32[32768]{0:T(1024)}) %all-reduce.8.cloned.1.call-update) | async-done | bytes 131088 | tf_op jit(solution)/shard_map/psum | solution.py:105
  721.7 70.8 %reduce-scatter.18.cloned.1.call-done = f32[16,384]{1,0:T(8,128)} async-done(((f32[16,6144]{1,0:T(8,128)}), f32[16,384]{1,0:T(8,128)}) %reduce-scatter.18.cloned.1.call-update) | async-done | bytes 24592 | tf_op jit(solution)/shard_map/reduce_scatter | solution.py:99
  832.6 62.8 %psum.110 = f32[]{:T(128)} all-reduce(f32[]{:T(128)} %multiply_reduce_fusion.8), channel_id=1, replica_groups=mesh['vox'=8,'fas'=16] {'vox','fas'}, use_global_device_ids=true, to_apply=%region_27.28 | all-reduce | flops 1 | bytes 8 | tf_op jit(solution)/shard_map/psum | solution.py:110
  926.8 69.0 %reduce-scatter.20.cloned.1.call-done = f32[16,384]{1,0:T(8,128)} async-done(((f32[16,6144]{1,0:T(8,128)}), f32[16,384]{1,0:T(8,128)}) %reduce-scatter.20.cloned.1.call-update) | async-done | bytes 24592 | tf_op jit(solution)/shard_map/reduce_scatter | solution.py:99
  1040.3 58.0 %all-reduce.10.cloned.1.call-done = f32[32768]{0:T(1024)} async-done(((f32[32768]{0:T(1024)}), f32[32768]{0:T(1024)}) %all-reduce.10.cloned.1.call-update) | async-done | bytes 131088 | tf_op jit(solution)/shard_map/psum | solution.py:105
  1129.6 70.8 %reduce-scatter.22.cloned.1.call-done = f32[16,384]{1,0:T(8,128)} async-done(((f32[16,6144]{1,0:T(8,128)}), f32[16,384]{1,0:T(8,128)}) %reduce-scatter.22.cloned.1.call-update) | async-done | bytes 24592 | tf_op jit(solution)/shard_map/reduce_scatter | solution.py:99
  1201.9 38.8 %psum.112 = f32[]{:T(128)} all-reduce(f32[]{:T(128)} %get-tuple-element.2456), channel_id=1, replica_groups=mesh['vox'=8,'fas'=16] {'fas'}, use_global_device_ids=true, to_apply=%region_36.37 | all-reduce | flops 1 | bytes 8 | tf_op jit(solution)/shard_map/psum | solution.py:109
  1240.6 62.7 %psum.113 = f32[]{:T(128)} all-reduce(f32[]{:T(128)} %multiply_reduce_fusion.7), channel_id=1, replica_groups=mesh['vox'=8,'fas'=16] {'vox','fas'}, use_global_device_ids=true, to_apply=%region_41.42 | all-reduce | flops 1 | bytes 8 | tf_op jit(solution)/shard_map/psum | solution.py:110
  1334.7 69.1 %reduce-scatter.24.cloned.1.call-done = f32[16,384]{1,0:T(8,128)} async-done(((f32[16,6144]{1,0:T(8,128)}), f32[16,384]{1,0:T(8,128)}) %reduce-scatter.24.cloned.1.call-update) | async-done | bytes 24592 | tf_op jit(solution)/shard_map/reduce_scatter | solution.py:99
  1448.3 57.9 %all-reduce.12.cloned.1.call-done = f32[32768]{0:T(1024)} async-done(((f32[32768]{0:T(1024)}), f32[32768]{0:T(1024)}) %all-reduce.12.cloned.1.call-update) | async-done | bytes 131088 | tf_op jit(solution)/shard_map/psum | solution.py:105
  1537.6 70.8 %reduce-scatter.26.cloned.1.call-done = f32[16,384]{1,0:T(8,128)} async-done(((f32[16,6144]{1,0:T(8,128)}), f32[16,384]{1,0:T(8,128)}) %reduce-scatter.26.cloned.1.call-update) | async-done | bytes 24592 | tf_op jit(solution)/shard_map/reduce_scatter | solution.py:99
  1648.6 62.8 %psum.116 = f32[]{:T(128)} all-reduce(f32[]{:T(128)} %multiply_reduce_fusion.6), channel_id=1, replica_groups=mesh['vox'=8,'fas'=16] {'vox','fas'}, use_global_device_ids=true, to_apply=%region_55.56 | all-reduce | flops 1 | bytes 8 | tf_op jit(solution)/shard_map/psum | solution.py:110
  1742.7 69.0 %reduce-scatter.28.cloned.1.call-done = f32[16,384]{1,0:T(8,128)} async-done(((f32[16,6144]{1,0:T(8,128)}), f32[16,384]{1,0:T(8,128)}) %reduce-scatter.28.cloned.1.call-update) | async-done | bytes 24592 | tf_op jit(solution)/shard_map/reduce_scatter | solution.py:99
  1856.2 58.0 %all-reduce.14.cloned.1.call-done = f32[32768]{0:T(1024)} async-done(((f32[32768]{0:T(1024)}), f32[32768]{0:T(1024)}) %all-reduce.14.cloned.1.call-update) | async-done | bytes 131088 | tf_op jit(solution)/shard_map/psum | solution.py:105
  1945.5 70.8 %reduce-scatter.30.cloned.1.call-done = f32[16,384]{1,0:T(8,128)} async-done(((f32[16,6144]{1,0:T(8,128)}), f32[16,384]{1,0:T(8,128)}) %reduce-scatter.30.cloned.1.call-update) | async-done | bytes 24592 | tf_op jit(solution)/shard_map/reduce_scatter | solution.py:99
  2056.5 62.7 %psum.119 = f32[]{:T(128)} all-reduce(f32[]{:T(128)} %multiply_reduce_fusion.5), channel_id=1, replica_groups=mesh['vox'=8,'fas'=16] {'vox','fas'}, use_global_device_ids=true, to_apply=%region_69.70 | all-reduce | flops 1 | bytes 8 | tf_op jit(solution)/shard_map/psum | solution.py:110
  2150.5 69.0 %reduce-scatter.32.cloned.1.call-done = f32[16,384]{1,0:T(8,128)} async-done(((f32[16,6144]{1,0:T(8,128)}), f32[16,384]{1,0:T(8,128)}) %reduce-scatter.32.cloned.1.call-update) | async-done | bytes 24592 | tf_op jit(solution)/shard_map/reduce_scatter | solution.py:99
  (241 shorter events, 1006.3 us)
Async XLA Ops:
  7.2 10.8 copy-start.15
  7.2 11.1 copy-start.14
  7.2 11.2 copy-start.16
  7.2 11.2 copy-start.11
  7.2 172.5 %reduce-scatter.12.cloned.1.call-start = ((), (), s32[]{:S(2)}) async-start(), calls=%async_computation.11 | async-start | bytes 417792 | tf_op jit(solution)/shard_map/reduce_scatter | solution.py:99
  18.5 58.1 %copy-start.17 = (s32[256]{0:T(256)S(1)}, s32[256]{0:T(256)}, u32[]{:S(2)}) copy-start(s32[256]{0:T(256)} %param.43) | copy-start | bytes 3076
  76.7 103.0 %copy-start.12 = (f32[16,384]{1,0:T(8,128)S(1)}, f32[16,384]{1,0:T(8,128)}, u32[]{:S(2)}) copy-start(f32[16,384]{1,0:T(8,128)} %param.40) | copy-start | bytes 73732
  104.6 0.7 copy-start.1
  105.4 176.9 %all-reduce.6.cloned.1.call-start = ((), (), s32[]{:S(2)}) async-start(), calls=%async_computation.12 | async-start | bytes 262144 | tf_op jit(solution)/shard_map/psum | solution.py:105
  224.2 160.4 %reduce-scatter.14.cloned.1.call-start = ((), (), s32[]{:S(2)}) async-start(), calls=%async_computation.13 | async-start | bytes 417792 | tf_op jit(solution)/shard_map/reduce_scatter | solution.py:99
  313.8 274.0 %reduce-scatter.16.cloned.1.call-start = ((), (), s32[]{:S(2)}) async-start(), calls=%async_computation.14 | async-start | bytes 417792 | tf_op jit(solution)/shard_map/reduce_scatter | solution.py:99
  518.7 171.6 %all-reduce.8.cloned.1.call-start = ((), (), s32[]{:S(2)}) async-start(), calls=%async_computation.15 | async-start | bytes 262144 | tf_op jit(solution)/shard_map/psum | solution.py:105
  632.2 160.2 %reduce-scatter.18.cloned.1.call-start = ((), (), s32[]{:S(2)}) async-start(), calls=%async_computation.16 | async-start | bytes 417792 | tf_op jit(solution)/shard_map/reduce_scatter | solution.py:99
  721.6 274.2 %reduce-scatter.20.cloned.1.call-start = ((), (), s32[]{:S(2)}) async-start(), calls=%async_computation.17 | async-start | bytes 417792 | tf_op jit(solution)/shard_map/reduce_scatter | solution.py:99
  926.8 171.5 %all-reduce.10.cloned.1.call-start = ((), (), s32[]{:S(2)}) async-start(), calls=%async_computation.18 | async-start | bytes 262144 | tf_op jit(solution)/shard_map/psum | solution.py:105
  1040.2 160.2 %reduce-scatter.22.cloned.1.call-start = ((), (), s32[]{:S(2)}) async-start(), calls=%async_computation.19 | async-start | bytes 417792 | tf_op jit(solution)/shard_map/reduce_scatter | solution.py:99
  1129.6 274.2 %reduce-scatter.24.cloned.1.call-start = ((), (), s32[]{:S(2)}) async-start(), calls=%async_computation.20 | async-start | bytes 417792 | tf_op jit(solution)/shard_map/reduce_scatter | solution.py:99
  1334.7 171.5 %all-reduce.12.cloned.1.call-start = ((), (), s32[]{:S(2)}) async-start(), calls=%async_computation.21 | async-start | bytes 262144 | tf_op jit(solution)/shard_map/psum | solution.py:105
  1448.2 160.2 %reduce-scatter.26.cloned.1.call-start = ((), (), s32[]{:S(2)}) async-start(), calls=%async_computation.22 | async-start | bytes 417792 | tf_op jit(solution)/shard_map/reduce_scatter | solution.py:99
  1537.5 274.2 %reduce-scatter.28.cloned.1.call-start = ((), (), s32[]{:S(2)}) async-start(), calls=%async_computation.23 | async-start | bytes 417792 | tf_op jit(solution)/shard_map/reduce_scatter | solution.py:99
  1742.7 171.5 %all-reduce.14.cloned.1.call-start = ((), (), s32[]{:S(2)}) async-start(), calls=%async_computation.24 | async-start | bytes 262144 | tf_op jit(solution)/shard_map/psum | solution.py:105
  1856.1 160.2 %reduce-scatter.30.cloned.1.call-start = ((), (), s32[]{:S(2)}) async-start(), calls=%async_computation.25 | async-start | bytes 417792 | tf_op jit(solution)/shard_map/reduce_scatter | solution.py:99
  1945.5 274.0 %reduce-scatter.32.cloned.1.call-start = ((), (), s32[]{:S(2)}) async-start(), calls=%async_computation.26 | async-start | bytes 417792 | tf_op jit(solution)/shard_map/reduce_scatter | solution.py:99
  2120.6 0.9 copy-start.13
  (10 other events, 7.5 us)
Sparse Core Ops, SparseCore 0:
  105.5 74.1 reduce-scatter.11
  224.3 57.9 all-reduce.5
  313.9 70.6 reduce-scatter.13
  518.8 68.9 reduce-scatter.15
  632.3 57.8 all-reduce.7
  721.7 70.6 reduce-scatter.17
  926.9 68.9 reduce-scatter.19
  1040.4 57.8 all-reduce.9
  1129.7 70.6 reduce-scatter.21
  1334.8 68.9 reduce-scatter.23
  1448.3 57.8 all-reduce.11
  1537.7 70.6 reduce-scatter.25
  1742.8 68.9 reduce-scatter.27
  1856.3 57.8 all-reduce.13
  1945.6 70.6 reduce-scatter.29
  2150.6 68.8 reduce-scatter.31
where the time goes:
time: 2240 us; the launch traced here: 2230 us
  waiting for transfers between devices  1060 us (47%)
  blocking collectives  625 us (28%)
  matrix products  275 us (12%)
  local copies, waits for them, and re-layouts  207 us (9%)
  other arithmetic  30.5 us (1%)
  between operations  22.5 us (1%)
    reduce_scatter x11, waiting for transfers between devices, collect(): lax.psum_scatter(partial_value, 'fas', scatter_dimension=1, tiled=True)  773 us
    psum x5, blocking collectives, local(): image_sq = lax.psum(image_local, ('vox', 'fas'))  314 us
    psum x5, waiting for transfers between devices, local(): lax.psum(backward_partial(whole_rows.reshape(vox_rows, BV, DIRS)), 'vox')  290 us
    psum x5, blocking collectives, local(): grad_sq = lax.psum(jnp.sum(projected * projected), 'fas')  194 us
    dot_general x11, matrix products, forward_accumulate(): jnp.einsum('kvj,kjd->kvd', scaled, atom_blk.astype(jnp.float32), precisio...  124 us
    all_gather x5, blocking collectives, local(): whole_rows = lax.all_gather(residual, 'fas', axis=1, tiled=True)  118 us
    dot_general x11, local copies, waits for them, and re-layouts, forward_accumulate(): jnp.einsum('kvj,kjd->kvd', scaled, atom_blk.astype(jnp.float32), precisio...  94.4 us
    dot_general x11, matrix products, forward_accumulate(): jnp.dot(selector.T, image_blk.reshape(group_size, row_width), precision=l...  81.8 us
  transfers between devices with their start and end apart: 16, of which 16 were waited for; matrix products, arithmetic and copies ran while one was open for 0% of the time, Pallas kernels for 0%

commit v1 on v0

--- a/solution.py
+++ b/solution.py
@@ -101,7 +101,29 @@
     weights = initial_weights
     residual = collect(forward_partial(weights)) - signal
     for sweep in range(ITERS):
-        whole_rows = lax.all_gather(residual, "fas", axis=1, tiled=True)
+        found_now, ready, arr_next = (
+            lax.axis_size("fas"),
+            lax.axis_index("fas"),
+            residual.shape[1],
+        )
+        views = tuple(((j, (j + 1) % found_now) for j in range(found_now)))
+        slots = tuple(((j, (j - 1) % found_now) for j in range(found_now)))
+        whole_rows = jnp.zeros(
+            (*residual.shape[:1], found_now * arr_next, *residual.shape[2:]), residual.dtype
+        )
+        tile_out = near = residual
+        whole_rows = lax.dynamic_update_slice_in_dim(whole_rows, residual, ready * arr_next, axis=1)
+        base_arr = found_now // 2
+        for dd in tuple(range(1, base_arr + 1)):
+            tile_out = lax.ppermute(tile_out, "fas", views)
+            whole_rows = lax.dynamic_update_slice_in_dim(
+                whole_rows, tile_out, (ready - dd) % found_now * arr_next, axis=1
+            )
+            if dd < found_now - base_arr:
+                near = lax.ppermute(near, "fas", slots)
+                whole_rows = lax.dynamic_update_slice_in_dim(
+                    whole_rows, near, (ready + dd) % found_now * arr_next, axis=1
+                )
         gradient = lax.psum(backward_partial(whole_rows.reshape(vox_rows, BV, DIRS)), "vox")
         projected = jnp.where((weights > 0) | (gradient < 0), gradient, 0.0)
         image_pred = collect(forward_partial(projected))

time: 2240 us -> 2400 us (1.071)
  starting transfers between devices: 0.65 us -> 190 us
  blocking collectives: 625 us -> 507 us
  waiting for transfers between devices: 1060 us -> 1150 us
    ppermute x0 -> x75, starting transfers between devices: none -> 189 us  [the longest x35 181 us: local(): near = lax.ppermute(near, 'fas', slots)]
    all_gather x5 -> x0, blocking collectives: 118 us -> none  [local(): whole_rows = lax.all_gather(residual, 'fas', axis=1, tiled=True)]
    ppermute x0 -> x75, waiting for transfers between devices: none -> 98.7 us  [the longest x40 98.6 us: local(): tile_out = lax.ppermute(tile_out, 'fas', views)]
  transfers between devices with their start and end apart: 16 -> 91, of which waited for: 16 -> 56; matrix products, arithmetic and copies ran while one was open for 0% -> 0% of each run, Pallas kernels for 0% -> 0%
where the time goes in v1:
time: 2400 us; the launch traced here: 2390 us
  waiting for transfers between devices  1150 us (48%)
  blocking collectives  507 us (21%)
  matrix products  276 us (12%)
  local copies, waits for them, and re-layouts  208 us (9%)
  starting transfers between devices  190 us (8%)
  other arithmetic  30.9 us (1%)
    reduce_scatter x11, waiting for transfers between devices, collect(): lax.psum_scatter(partial_value, 'fas', scatter_dimension=1, tiled=True)  773 us
    psum x5, blocking collectives, local(): image_sq = lax.psum(image_local, ('vox', 'fas'))  314 us
    psum x5, waiting for transfers between devices, local(): lax.psum(backward_partial(whole_rows.reshape(vox_rows, BV, DIRS)), 'vox')  278 us
    psum x5, blocking collectives, local(): grad_sq = lax.psum(jnp.sum(projected * projected), 'fas')  194 us
    ppermute x35, starting transfers between devices, local(): near = lax.ppermute(near, 'fas', slots)  181 us
    dot_general x11, matrix products, forward_accumulate(): jnp.einsum('kvj,kjd->kvd', scaled, atom_blk.astype(jnp.float32), precisio...  124 us
    ppermute x40, waiting for transfers between devices, local(): tile_out = lax.ppermute(tile_out, 'fas', views)  98.6 us
    dot_general x11, local copies, waits for them, and re-layouts, forward_accumulate(): jnp.einsum('kvj,kjd->kvd', scaled, atom_blk.astype(jnp.float32), precisio...  94.1 us
  transfers between devices with their start and end apart: 91, of which 56 were waited for; matrix products, arithmetic and copies ran while one was open for 0% of the time, Pallas kernels for 0%

profile of v1, /device:TPU:0, one launch (start us, length us, event | category | flops | bytes accessed | tf_op | source)
XLA Modules:
  0.0 2387.6 jit_solution(17469126836601933745)
XLA Ops:
  20.8 57.4 %gather_fusion = bf16[16384,96]{1,0:T(8,128)(2,1)} fusion(bf16[360,96]{1,0:T(8,128)(2,1)S(1)} %copy.28, s32[16384]{0:T(1024)S(1)} %broadcast_clamp_fusion), kind=kCustom, calls=%fused_computation | custom fusion | bytes 6356992 | tf_op jit(solution)/shard_map/gather | solution.py:30
  107.0 74.3 %reduce-scatter.12.cloned.1.call-done = f32[16,384]{1,0:T(8,128)} async-done(((f32[16,6144]{1,0:T(8,128)}), f32[16,384]{1,0:T(8,128)}) %reduce-scatter.12.cloned.1.call-update) | async-done | bytes 24592 | tf_op jit(solution)/shard_map/reduce_scatter | solution.py:99
  260.4 55.6 %all-reduce.6.cloned.1.call-done = f32[32768]{0:T(1024)} async-done(((f32[32768]{0:T(1024)}), f32[32768]{0:T(1024)}) %all-reduce.6.cloned.1.call-update) | async-done | bytes 131088 | tf_op jit(solution)/shard_map/psum | solution.py:127
  347.4 70.8 %reduce-scatter.14.cloned.1.call-done = f32[16,384]{1,0:T(8,128)} async-done(((f32[16,6144]{1,0:T(8,128)}), f32[16,384]{1,0:T(8,128)}) %reduce-scatter.14.cloned.1.call-update) | async-done | bytes 24592 | tf_op jit(solution)/shard_map/reduce_scatter | solution.py:99
  419.5 38.8 %psum.106 = f32[]{:T(128)} all-reduce(f32[]{:T(128)} %get-tuple-element.2468), channel_id=1, replica_groups=mesh['vox'=8,'fas'=16] {'fas'}, use_global_device_ids=true, to_apply=%region_8.9 | all-reduce | flops 1 | bytes 8 | tf_op jit(solution)/shard_map/psum | solution.py:131
  458.3 62.7 %psum.107 = f32[]{:T(128)} all-reduce(f32[]{:T(128)} %multiply_reduce_fusion.9), channel_id=1, replica_groups=mesh['vox'=8,'fas'=16] {'vox','fas'}, use_global_device_ids=true, to_apply=%region_13.14 | all-reduce | flops 1 | bytes 8 | tf_op jit(solution)/shard_map/psum | solution.py:132
  552.2 69.1 %reduce-scatter.16.cloned.1.call-done = f32[16,384]{1,0:T(8,128)} async-done(((f32[16,6144]{1,0:T(8,128)}), f32[16,384]{1,0:T(8,128)}) %reduce-scatter.16.cloned.1.call-update) | async-done | bytes 24592 | tf_op jit(solution)/shard_map/reduce_scatter | solution.py:99
  699.9 55.7 %all-reduce.8.cloned.1.call-done = f32[32768]{0:T(1024)} async-done(((f32[32768]{0:T(1024)}), f32[32768]{0:T(1024)}) %all-reduce.8.cloned.1.call-update) | async-done | bytes 131088 | tf_op jit(solution)/shard_map/psum | solution.py:127
  786.9 70.8 %reduce-scatter.18.cloned.1.call-done = f32[16,384]{1,0:T(8,128)} async-done(((f32[16,6144]{1,0:T(8,128)}), f32[16,384]{1,0:T(8,128)}) %reduce-scatter.18.cloned.1.call-update) | async-done | bytes 24592 | tf_op jit(solution)/shard_map/reduce_scatter | solution.py:99
  897.9 62.7 %psum.110 = f32[]{:T(128)} all-reduce(f32[]{:T(128)} %multiply_reduce_fusion.8), channel_id=1, replica_groups=mesh['vox'=8,'fas'=16] {'vox','fas'}, use_global_device_ids=true, to_apply=%region_27.28 | all-reduce | flops 1 | bytes 8 | tf_op jit(solution)/shard_map/psum | solution.py:132
  991.8 69.0 %reduce-scatter.20.cloned.1.call-done = f32[16,384]{1,0:T(8,128)} async-done(((f32[16,6144]{1,0:T(8,128)}), f32[16,384]{1,0:T(8,128)}) %reduce-scatter.20.cloned.1.call-update) | async-done | bytes 24592 | tf_op jit(solution)/shard_map/reduce_scatter | solution.py:99
  1139.5 55.6 %all-reduce.10.cloned.1.call-done = f32[32768]{0:T(1024)} async-done(((f32[32768]{0:T(1024)}), f32[32768]{0:T(1024)}) %all-reduce.10.cloned.1.call-update) | async-done | bytes 131088 | tf_op jit(solution)/shard_map/psum | solution.py:127
  1226.5 70.8 %reduce-scatter.22.cloned.1.call-done = f32[16,384]{1,0:T(8,128)} async-done(((f32[16,6144]{1,0:T(8,128)}), f32[16,384]{1,0:T(8,128)}) %reduce-scatter.22.cloned.1.call-update) | async-done | bytes 24592 | tf_op jit(solution)/shard_map/reduce_scatter | solution.py:99
  1337.5 62.7 %psum.113 = f32[]{:T(128)} all-reduce(f32[]{:T(128)} %multiply_reduce_fusion.7), channel_id=1, replica_groups=mesh['vox'=8,'fas'=16] {'vox','fas'}, use_global_device_ids=true, to_apply=%region_41.42 | all-reduce | flops 1 | bytes 8 | tf_op jit(solution)/shard_map/psum | solution.py:132
  1431.3 69.0 %reduce-scatter.24.cloned.1.call-done = f32[16,384]{1,0:T(8,128)} async-done(((f32[16,6144]{1,0:T(8,128)}), f32[16,384]{1,0:T(8,128)}) %reduce-scatter.24.cloned.1.call-update) | async-done | bytes 24592 | tf_op jit(solution)/shard_map/reduce_scatter | solution.py:99
  1579.1 55.7 %all-reduce.12.cloned.1.call-done = f32[32768]{0:T(1024)} async-done(((f32[32768]{0:T(1024)}), f32[32768]{0:T(1024)}) %all-reduce.12.cloned.1.call-update) | async-done | bytes 131088 | tf_op jit(solution)/shard_map/psum | solution.py:127
  1666.1 70.8 %reduce-scatter.26.cloned.1.call-done = f32[16,384]{1,0:T(8,128)} async-done(((f32[16,6144]{1,0:T(8,128)}), f32[16,384]{1,0:T(8,128)}) %reduce-scatter.26.cloned.1.call-update) | async-done | bytes 24592 | tf_op jit(solution)/shard_map/reduce_scatter | solution.py:99
  1777.0 62.7 %psum.116 = f32[]{:T(128)} all-reduce(f32[]{:T(128)} %multiply_reduce_fusion.6), channel_id=1, replica_groups=mesh['vox'=8,'fas'=16] {'vox','fas'}, use_global_device_ids=true, to_apply=%region_55.56 | all-reduce | flops 1 | bytes 8 | tf_op jit(solution)/shard_map/psum | solution.py:132
  1870.9 69.0 %reduce-scatter.28.cloned.1.call-done = f32[16,384]{1,0:T(8,128)} async-done(((f32[16,6144]{1,0:T(8,128)}), f32[16,384]{1,0:T(8,128)}) %reduce-scatter.28.cloned.1.call-update) | async-done | bytes 24592 | tf_op jit(solution)/shard_map/reduce_scatter | solution.py:99
  2018.6 55.7 %all-reduce.14.cloned.1.call-done = f32[32768]{0:T(1024)} async-done(((f32[32768]{0:T(1024)}), f32[32768]{0:T(1024)}) %all-reduce.14.cloned.1.call-update) | async-done | bytes 131088 | tf_op jit(solution)/shard_map/psum | solution.py:127
  2105.7 70.8 %reduce-scatter.30.cloned.1.call-done = f32[16,384]{1,0:T(8,128)} async-done(((f32[16,6144]{1,0:T(8,128)}), f32[16,384]{1,0:T(8,128)}) %reduce-scatter.30.cloned.1.call-update) | async-done | bytes 24592 | tf_op jit(solution)/shard_map/reduce_scatter | solution.py:99
  2177.8 38.8 %psum.118 = f32[]{:T(128)} all-reduce(f32[]{:T(128)} %get-tuple-element.2452), channel_id=1, replica_groups=mesh['vox'=8,'fas'=16] {'fas'}, use_global_device_ids=true, to_apply=%region_64.65 | all-reduce | flops 1 | bytes 8 | tf_op jit(solution)/shard_map/psum | solution.py:131
  2216.6 62.7 %psum.119 = f32[]{:T(128)} all-reduce(f32[]{:T(128)} %multiply_reduce_fusion.5), channel_id=1, replica_groups=mesh['vox'=8,'fas'=16] {'vox','fas'}, use_global_device_ids=true, to_apply=%region_69.70 | all-reduce | flops 1 | bytes 8 | tf_op jit(solution)/shard_map/psum | solution.py:132
  2310.4 69.1 %reduce-scatter.32.cloned.1.call-done = f32[16,384]{1,0:T(8,128)} async-done(((f32[16,6144]{1,0:T(8,128)}), f32[16,384]{1,0:T(8,128)}) %reduce-scatter.32.cloned.1.call-update) | async-done | bytes 24592 | tf_op jit(solution)/shard_map/reduce_scatter | solution.py:99
  (461 shorter events, 1178.4 us)
Async XLA Ops:
  7.2 174.0 %reduce-scatter.12.cloned.1.call-start = ((), (), s32[]{:S(2)}) async-start(), calls=%async_computation.11 | async-start | bytes 417792 | tf_op jit(solution)/shard_map/reduce_scatter | solution.py:99
  106.9 209.1 %all-reduce.6.cloned.1.call-start = ((), (), s32[]{:S(2)}) async-start(), calls=%async_computation.12 | async-start | bytes 262144 | tf_op jit(solution)/shard_map/psum | solution.py:127
  225.3 7.7 collective-permute-start.13
  232.4 7.7 collective-permute-start.14
  260.3 157.8 %reduce-scatter.14.cloned.1.call-start = ((), (), s32[]{:S(2)}) async-start(), calls=%async_computation.13 | async-start | bytes 417792 | tf_op jit(solution)/shard_map/reduce_scatter | solution.py:99
  347.3 273.9 %reduce-scatter.16.cloned.1.call-start = ((), (), s32[]{:S(2)}) async-start(), calls=%async_computation.14 | async-start | bytes 417792 | tf_op jit(solution)/shard_map/reduce_scatter | solution.py:99
  552.1 203.5 %all-reduce.8.cloned.1.call-start = ((), (), s32[]{:S(2)}) async-start(), calls=%async_computation.15 | async-start | bytes 262144 | tf_op jit(solution)/shard_map/psum | solution.py:127
  650.7 7.6 collective-permute-start.24
  657.8 7.5 collective-permute-start.25
  699.9 157.9 %reduce-scatter.18.cloned.1.call-start = ((), (), s32[]{:S(2)}) async-start(), calls=%async_computation.16 | async-start | bytes 417792 | tf_op jit(solution)/shard_map/reduce_scatter | solution.py:99
  786.9 273.9 %reduce-scatter.20.cloned.1.call-start = ((), (), s32[]{:S(2)}) async-start(), calls=%async_computation.17 | async-start | bytes 417792 | tf_op jit(solution)/shard_map/reduce_scatter | solution.py:99
  991.7 203.4 %all-reduce.10.cloned.1.call-start = ((), (), s32[]{:S(2)}) async-start(), calls=%async_computation.18 | async-start | bytes 262144 | tf_op jit(solution)/shard_map/psum | solution.py:127
  1090.3 7.6 collective-permute-start.39
  1139.5 157.8 %reduce-scatter.22.cloned.1.call-start = ((), (), s32[]{:S(2)}) async-start(), calls=%async_computation.19 | async-start | bytes 417792 | tf_op jit(solution)/shard_map/reduce_scatter | solution.py:99
  1226.5 273.9 %reduce-scatter.24.cloned.1.call-start = ((), (), s32[]{:S(2)}) async-start(), calls=%async_computation.20 | async-start | bytes 417792 | tf_op jit(solution)/shard_map/reduce_scatter | solution.py:99
  1431.3 203.5 %all-reduce.12.cloned.1.call-start = ((), (), s32[]{:S(2)}) async-start(), calls=%async_computation.21 | async-start | bytes 262144 | tf_op jit(solution)/shard_map/psum | solution.py:127
  1529.8 7.6 collective-permute-start.54
  1536.9 7.5 collective-permute-start.55
  1579.0 157.9 %reduce-scatter.26.cloned.1.call-start = ((), (), s32[]{:S(2)}) async-start(), calls=%async_computation.22 | async-start | bytes 417792 | tf_op jit(solution)/shard_map/reduce_scatter | solution.py:99
  1666.0 273.9 %reduce-scatter.28.cloned.1.call-start = ((), (), s32[]{:S(2)}) async-start(), calls=%async_computation.23 | async-start | bytes 417792 | tf_op jit(solution)/shard_map/reduce_scatter | solution.py:99
  1870.9 203.4 %all-reduce.14.cloned.1.call-start = ((), (), s32[]{:S(2)}) async-start(), calls=%async_computation.24 | async-start | bytes 262144 | tf_op jit(solution)/shard_map/psum | solution.py:127
  1969.4 7.6 collective-permute-start.69
  2018.6 157.9 %reduce-scatter.30.cloned.1.call-start = ((), (), s32[]{:S(2)}) async-start(), calls=%async_computation.25 | async-start | bytes 417792 | tf_op jit(solution)/shard_map/reduce_scatter | solution.py:99
  2105.6 273.9 %reduce-scatter.32.cloned.1.call-start = ((), (), s32[]{:S(2)}) async-start(), calls=%async_computation.26 | async-start | bytes 417792 | tf_op jit(solution)/shard_map/reduce_scatter | solution.py:99
  (83 other events, 683.6 us)
Sparse Core Ops, SparseCore 0:
  107.0 74.1 reduce-scatter.11
  260.4 55.5 all-reduce.5
  347.4 70.6 reduce-scatter.13
  552.2 68.9 reduce-scatter.15
  700.0 55.5 all-reduce.7
  787.0 70.6 reduce-scatter.17
  991.8 68.9 reduce-scatter.19
  1139.6 55.5 all-reduce.9
  1226.6 70.6 reduce-scatter.21
  1431.4 68.9 reduce-scatter.23
  1579.1 55.5 all-reduce.11
  1666.2 70.6 reduce-scatter.25
  1871.0 68.8 reduce-scatter.27
  2018.7 55.5 all-reduce.13
  2105.7 70.6 reduce-scatter.29
  2310.6 68.9 reduce-scatter.31
